TPU v7x, 256 devices: a whole 4x4x8 slice. The times are simulated.
256 devices in a mesh: slab: 4 (over z_lo, core), modes: 64 (over z_hi, y, x).
Axes of the slice: x: 4, y: 4, z: 8 (z_hi: 4, z_lo: 2; z = z_hi * 2 + z_lo), core: 2. Of those that a mesh axis runs over, the one named last changes fastest.
Arguments:
- occupation_prior: float32 [512, 32768], P('slab', 'modes'), may hold values from -6 to 6
- coupling: bfloat16 [256, 64, 128, 128], P('modes'), may hold values from -0.1875 to 0.1875
- pattern: int32 [256, 64], P('modes'), may hold values from 0 to 3
- pseudo_weights: float32 [32768], P('modes'), may hold values from -0.03125 to 0.03125
- equilibrium_slope: float32 [32768], replicated, may hold values from 0.3 to 3
- direction: int32 [256], P('modes'), may hold values from 0 to 1
- stream_rate: float32 [32768], P('modes'), may hold values from 0.15 to 0.95
- inscatter: float32 [256, 128, 128], P('modes'), may hold values from -0.125 to 0.125
- inflow_low: float32 [4, 32768], P(None, 'modes'), may hold values from -6 to 6
- inflow_high: float32 [4, 32768], P(None, 'modes'), may hold values from -6 to 6
- front_of_row: int32 [16], replicated, may hold values from 0 to 3
Outputs:
- swept: float32 [512, 32768], P('slab', 'modes')
Inputs may be any that keep to these rules, and one draw needn't show every extreme that they name: `pattern`: each entry names one of the 4 blocks of a group.
All inputs are finite; a program needn't handle non-finite values.
Results may differ from a plain program's by a relative error of at most 0.002.
Values sent between devices are 32-bit elements; how exact they have to be, the bound alone decides.
No kernel may reach another device: no remote copies, remote signals or barrier semaphores. Data moves between devices by JAX's collectives and lax.ppermute only.
A program may use at most 128 MiB of HBM per device.

v0:
```python
import jax
import jax.numpy as jnp
from jax import lax
from jax.sharding import PartitionSpec as P

BLK = 128
SHELL = 4


def shifted(block, axis, distance):
    devices = range(lax.axis_size(axis))
    route = [(i - distance, i) for i in devices if i - distance in devices]
    return lax.ppermute(block, axis, route)


def advance(face_now, power_matrix, shift_amount):
    return (
        jnp.einsum("ybk,bkl->ybl", face_now, power_matrix, precision=lax.Precision.HIGHEST)
        + shift_amount
    )


def per_device(
    occupation_prior,
    coupling,
    pattern,
    pseudo_weights,
    equilibrium_slope,
    direction,
    stream_rate,
    inscatter,
    inflow_low,
    inflow_high,
    front_of_row,
):
    cell_count, local_width = occupation_prior.shape
    group_count = coupling.shape[1]
    lateral = front_of_row.shape[0]
    rounded = occupation_prior.astype(jnp.bfloat16).reshape(cell_count, SHELL, BLK)
    products = jnp.einsum("cbk,bgkl->bcgl", rounded, coupling, preferred_element_type=jnp.float32)
    selected = pattern[:, :, None] == jnp.arange(SHELL, dtype=jnp.int32)[None, None, :]
    partial_term = jnp.sum(
        jnp.where(selected[:, None, :, :, None], products[:, :, :, None, :], 0.0), axis=0
    )
    partial_term = partial_term.reshape(cell_count, group_count * local_width)
    branch_pseudo_warmth = jnp.sum(occupation_prior * pseudo_weights[None, :], axis=1)
    collided_branches = lax.psum_scatter(partial_term, "modes", scatter_dimension=1, tiled=True)
    local_specific_warmth = lax.dynamic_slice_in_dim(
        equilibrium_slope, lax.axis_index("modes") * local_width, local_width
    )
    pseudo_warmth_sum = lax.psum(branch_pseudo_warmth, "modes")
    gain_contribution = (
        collided_branches + pseudo_warmth_sum[:, None] * local_specific_warmth[None, :]
    )
    slab_cells = cell_count // lateral
    source_cells = gain_contribution.reshape(slab_cells, lateral, SHELL, BLK)
    forward_mask = (direction == 1)[None, None, :, None]
    ordered = jnp.where(forward_mask, source_cells, source_cells[::-1])
    rate_table = stream_rate.reshape(SHELL, BLK)
    transfer = jnp.eye(BLK, dtype=jnp.float32)[None] + inscatter
    step_matrix = rate_table[:, :, None] * transfer

    def local_sweep(carry, layer_source):
        previous, power_matrix = carry
        previous = jnp.einsum(
            "ybk,bkl->ybl",
            layer_source + rate_table * previous,
            transfer,
            precision=lax.Precision.HIGHEST,
        )
        following = jnp.einsum(
            "bkl,blm->bkm", power_matrix, step_matrix, precision=lax.Precision.HIGHEST
        )
        return ((previous, following), (previous, power_matrix))

    start_carry = (jnp.zeros((lateral, SHELL, BLK), jnp.float32), step_matrix)
    _, (particular, powers) = lax.scan(local_sweep, start_carry, ordered)
    row_picks = (
        front_of_row[:, None] == jnp.arange(inflow_low.shape[0], dtype=jnp.int32)[None, :]
    ).astype(jnp.float32)
    wall_low = jnp.dot(row_picks, inflow_low, precision=lax.Precision.HIGHEST).reshape(
        lateral, SHELL, BLK
    )
    wall_high = jnp.dot(row_picks, inflow_high, precision=lax.Precision.HIGHEST).reshape(
        lateral, SHELL, BLK
    )
    last_power = powers[-1]
    last_part = particular[-1]
    index_of_slab = lax.axis_index("slab")
    slab_count = lax.axis_size("slab")
    at_first = index_of_slab == 0
    at_final = index_of_slab == slab_count - 1

    def relay(turn_index, face_pair):
        low_face, high_face = face_pair
        moved_up = shifted(advance(low_face, last_power, last_part), "slab", 1)
        moved_down = shifted(advance(high_face, last_power, last_part), "slab", -1)
        return (jnp.where(at_first, wall_low, moved_up), jnp.where(at_final, wall_high, moved_down))

    from_low, from_high = lax.fori_loop(0, slab_count - 1, relay, (wall_low, wall_high))
    inflow = jnp.where(forward_mask[0], from_low, from_high)
    layers = particular + jnp.einsum(
        "ybk,xbkl->xybl", inflow, powers, precision=lax.Precision.HIGHEST
    )
    result = jnp.where(forward_mask, layers, layers[::-1])
    return result.reshape(cell_count, local_width)


def solution(mesh):
    placed = (
        P("slab", "modes"),
        P("modes", None, None, None),
        P("modes", None),
        P("modes"),
        P(),
        P("modes"),
        P("modes"),
        P("modes", None, None),
        P(None, "modes"),
        P(None, "modes"),
        P(),
    )
    return jax.shard_map(
        per_device, mesh=mesh, in_specs=placed, out_specs=P("slab", "modes"), check_vma=False
    )
```

profile of v0, /device:TPU:1, one launch (start us, length us, event | category | flops | bytes accessed | tf_op | source)
XLA Modules:
  0.0 551.1 jit_solution(12531510711625178505)
XLA Ops:
  6.5 1.2 multiply_reduce_fusion
  7.7 5.7 %fusion.15 = f32[4,128,64,128]{3,1,2,0:T(8,128)S(1)} fusion(bf16[4,64,128,128]{3,2,1,0:T(8,128)(2,1)} %param.16, bf16[128,4,128,1]{2,1,0,3:T(4,128)(2,1)S(1)} %bitcast.92), kind=kOutput, calls=%fused_computation.27 | convolution fusion | flops 1073741824 | bytes 25296896 | tf_op jit(solution)/shard_map/cbk,bgkl->bcgl/dot_general | solution.py:40
  13.5 11.7 %copy.46 = f32[4,128,64,128]{3,2,1,0:T(8,128)} copy(f32[4,128,64,128]{3,1,2,0:T(8,128)S(1)} %fusion.15) | data formatting | bytes 33554432 | tf_op jit(solution)/shard_map/cbk,bgkl->bcgl/dot_general | solution.py:40
  25.2 26.4 %select_reduce_fusion = f32[128,64,4,128]{3,1,2,0:T(8,128)} fusion(f32[4,128,64,128]{3,2,1,0:T(8,128)} %copy.46, pred[4,64,4]{1,2,0:T(4,128)(4,1)S(1)} %iota_compare_fusion.4), kind=kLoop, calls=%fused_computation.14 | loop fusion | flops 29360128 | bytes 33555456 | tf_op jit(solution)/shard_map/reduce_sum | solution.py:42
  51.6 17.5 %copy.47 = f32[128,64,4,128]{0,3,2,1:T(8,128)} copy(f32[128,64,4,128]{3,1,2,0:T(8,128)} %select_reduce_fusion) | data formatting | bytes 33554432 | tf_op jit(solution)/shard_map/reduce_sum | solution.py:42
  69.2 0.9 copy-done.1
  70.3 0.2 convolution_bitcast_fusion.2
  70.5 0.2 convolution_bitcast_fusion.3
  70.7 0.8 dynamic_slice.7
  71.5 188.3 %psum.7 = f32[128]{0:T(128)S(1)} all-reduce(f32[128]{0:T(128)S(1)} %get-tuple-element.217), channel_id=1, replica_groups=mesh['slab'=4,'modes'=64] {'modes'}, use_global_device_ids=true, to_apply=%region_3.4 | all-reduce | flops 128 | bytes 1024 | tf_op jit(solution)/shard_map/psum | solution.py:51
  259.8 233.6 %reduce-scatter.2.cloned.1.call-done = f32[128,512]{0,1:T(8,128)} async-done(((f32[128,32768]{0,1:T(8,128)}), f32[128,512]{0,1:T(8,128)}) %reduce-scatter.2.cloned.1.call-update) | async-done | bytes 262160 | tf_op jit(solution)/shard_map/reduce_scatter | solution.py:47
  493.4 1.1 multiply_add_fusion
  494.9 11.5 %while.28 = (s32[]{:T(128)}, f32[16,4,128]{2,0,1:T(8,128)S(1)}, f32[4,128,128]{2,1,0:T(8,128)S(1)}, f32[8,16,4,128]{3,1,2,0:T(8,128)}, f32[8,4,128,128]{3,2,1,0:...) while((s32[]{:T(128)}, f32[16,4,128]{2,0,1:T(8,128)S(1)}, ...), condition=%wide.region_5.6_spmd, body=%wide.region_4.5_spmd.sunk | while | flops 113262592 | bytes 2296937 | solution.py:77
  494.9 1.0 bitcast_dynamic-update-slice_fusion.4
  495.9 0.4 fusion.47
  496.3 1.0 bitcast_dynamic-update-slice_fusion.4
  497.3 0.4 fusion.47
  497.8 1.0 bitcast_dynamic-update-slice_fusion.4
  498.8 0.4 fusion.47
  499.2 1.0 bitcast_dynamic-update-slice_fusion.4
  500.2 0.4 fusion.47
  500.7 1.0 bitcast_dynamic-update-slice_fusion.4
  501.7 0.4 fusion.47
  502.1 1.0 bitcast_dynamic-update-slice_fusion.4
  503.1 0.4 fusion.47
  503.5 1.0 bitcast_dynamic-update-slice_fusion.4
  504.5 0.4 fusion.47
  505.0 1.0 bitcast_dynamic-update-slice_fusion.4
  506.0 0.4 fusion.47
  506.4 0.8 slice_bitcast_fusion.1
  507.2 33.9 %while.29 = (s32[]{:T(128)}, f32[16,4,128]{2,0,1:T(8,128)S(1)}, f32[16,4,128]{2,0,1:T(8,128)S(1)}, pred[]{:T(512)}, f32[4,128,128]{2,1,0:T(8,128)S(1)}, /*index=...) while((s32[]{:T(128)}, f32[16,4,128]{2,0,1:T(8,128)S(1)}, ...), condition=%wide.region_7.8_spmd, body=%wide.region_6.7_spmd.sunk | while | flops 25198592 | bytes 1179831 | solution.py:100
  507.2 0.3 fusion.52
  507.5 11.3 %collective-permute-start = (f32[16,4,128]{2,0,1:T(8,128)S(1)}, f32[16,4,128]{2,0,1:T(8,128)S(1)}, u32[]{:S(2)}, u32[]{:S(2)}) collective-permute-start(f32[16,4,128]{2,0,1:T(8,128)S(1)} %fusion.52), channel_id=1, source_target_pairs={{0,64},{64,128},{128,192},{1,65},{65,129},{129,193},{2,66},{66,130... | collective-permute-start | bytes 98312 | tf_op jit(solution)/shard_map/while/body/eval_jaxpr/ppermute | solution.py:13
  518.8 0.3 fusion.53
  519.1 5.5 collective-permute-start.1
  524.6 0.8 collective-permute-done.1
  525.5 0.3 fusion.52
  525.8 1.9 collective-permute-start
  527.7 0.3 fusion.53
  528.1 2.4 collective-permute-start.1
  530.5 2.8 collective-permute-done.1
  533.3 0.3 fusion.52
  533.6 1.9 collective-permute-start
  535.6 0.3 fusion.53
  535.9 2.4 collective-permute-start.1
  538.3 2.8 collective-permute-done.1
  541.1 2.2 fusion.12
  543.6 0.7 copy.79
  (67 shorter events, 1.3 us)
Async XLA Ops:
  6.5 63.7 %copy-start = (f32[4,512]{1,0:T(4,128)S(1)}, f32[4,512]{1,0:T(4,128)}, u32[]{:S(2)}) copy-start(f32[4,512]{1,0:T(4,128)} %param.24) | copy-start | bytes 24580
  6.5 486.9 %reduce-scatter.2.cloned.1.call-start = ((), (), s32[]{:S(2)}) async-start(), calls=%async_computation.1 | async-start | bytes 17039360 | tf_op jit(solution)/shard_map/reduce_scatter | solution.py:47
  13.5 11.7 %copy-start.3 = (s32[4,64]{1,0:T(4,128)S(1)}, s32[4,64]{1,0:T(4,128)}, u32[]{:S(2)}) copy-start(s32[4,64]{1,0:T(4,128)} %param.17) | copy-start | bytes 3076
  69.1 0.9 copy-start.1
  69.1 1.0 copy-start.2
  69.2 1.1 copy-start.5
  69.2 1.3 copy-start.4
  69.2 190.7 %copy-start.6 = (s32[4]{0:T(128)S(1)}, s32[4]{0:T(128)}, u32[]{:S(2)}) copy-start(s32[4]{0:T(128)} %param.20) | copy-start | bytes 52
  507.5 17.1 %collective-permute-start = (f32[16,4,128]{2,0,1:T(8,128)S(1)}, f32[16,4,128]{2,0,1:T(8,128)S(1)}, u32[]{:S(2)}, u32[]{:S(2)}) collective-permute-start(f32[16,4,128]{2,0,1:T(8,128)S(1)} %fusion.52), channel_id=1, source_target_pairs={{0,64},{64,128},{128,192},{1,65},{65,129},{129,193},{2,66},{66,130... | collective-permute-start | bytes 98312 | tf_op jit(solution)/shard_map/while/body/eval_jaxpr/ppermute | solution.py:13
  519.1 6.3 %collective-permute-start.1 = (f32[16,4,128]{2,0,1:T(8,128)S(1)}, f32[16,4,128]{2,0,1:T(8,128)S(1)}, u32[]{:S(2)}, u32[]{:S(2)}) collective-permute-start(f32[16,4,128]{2,0,1:T(8,128)S(1)} %fusion.53), channel_id=1, source_target_pairs={{64,0},{128,64},{192,128},{65,1},{129,65},{193,129},{66,2},{130,66... | collective-permute-start | bytes 98312 | tf_op jit(solution)/shard_map/while/body/eval_jaxpr/ppermute | solution.py:13
  525.8 4.7 collective-permute-start
  528.1 5.2 collective-permute-start.1
  533.6 4.7 collective-permute-start
  535.9 5.2 collective-permute-start.1
Sparse Core Ops, SparseCore 0:
  69.3 424.0 reduce-scatter.1
where the time goes:
time: 552 us; the launch traced here: 551 us
  waiting for transfers between devices  240 us (43%)
  blocking collectives  188 us (34%)
  local copies, waits for them, and re-layouts  33.3 us (6%)
  other arithmetic  29 us (5%)
  starting transfers between devices  25.3 us (5%)
  matrix products  21.2 us (4%)
  between operations  13.6 us (2%)
    reduce_scatter x1, waiting for transfers between devices, per_device(): lax.psum_scatter(partial_term, 'modes', scatter_dimension=1, tiled=True)  234 us
    psum x1, blocking collectives, per_device(): pseudo_warmth_sum = lax.psum(branch_pseudo_warmth, 'modes')  188 us
    reduce_sum x1, other arithmetic, per_device(): jnp.sum(jnp.where(selected[:, None, :, :, None], products[:, :, :, None,...  26.4 us
    ppermute x6, starting transfers between devices, shifted(): return lax.ppermute(block, axis, route)  25.3 us
    reduce_sum x1, local copies, waits for them, and re-layouts, per_device(): jnp.sum(jnp.where(selected[:, None, :, :, None], products[:, :, :, None,...  17.5 us
    dot_general x1, local copies, waits for them, and re-layouts, per_device(): jnp.einsum('cbk,bgkl->bcgl', rounded, coupling, preferred_element_type=jn...  11.7 us
  transfers between devices with their start and end apart: 7, of which 4 were waited for; matrix products, arithmetic and copies ran while one was open for 0% of the time, Pallas kernels for 0%

commit v1 on v0

v1 whole, which is shorter than its diff:
```python
import functools

import jax
import jax.numpy as jnp
from jax import lax
from jax.experimental import pallas as pl
from jax.experimental.pallas import tpu as pltpu
from jax.sharding import PartitionSpec as P

BLK = 128
SHELL = 4
ZN = 4
PLANE = 16
PER_STEP = 4
LAYERS = 8
LATERAL = 16
WIDTH = SHELL * BLK
CELL = LAYERS * LATERAL
HIGH = lax.Precision.HIGHEST
PLANES = [[z * PLANE + i for i in range(PLANE)] for z in range(ZN)]


def z_route(step):
    return [
        (z * PLANE + i, ((z + step) % ZN) * PLANE + i) for z in range(ZN) for i in range(PLANE)
    ]


def partial_kernel(steps_ref, pattern_ref, x_ref, weight_ref, slope_ref, coupling_ref, out_ref, rounded, warmth):
    step = pl.program_id(0)

    @pl.when(step == 0)
    def _():
        prior = x_ref[...]
        rounded[...] = prior.astype(jnp.bfloat16)
        total = jnp.sum(prior * weight_ref[...], axis=1, keepdims=True)
        warmth[...] = jnp.broadcast_to(total, warmth.shape)

    first = steps_ref[step] * PER_STEP
    heat = warmth[...]
    for g in range(PER_STEP):
        for t in range(SHELL):
            lanes = pl.ds(t * BLK, BLK)
            out_ref[0, g, :, lanes] = heat * slope_ref[pl.ds(g, 1), lanes]
        for b in range(SHELL):
            product = jnp.dot(
                rounded[:, pl.ds(b * BLK, BLK)],
                coupling_ref[b, g],
                preferred_element_type=jnp.float32,
            )
            where = pattern_ref[b, first + g]
            lanes = pl.ds(pl.multiple_of(where * BLK, BLK), BLK)
            out_ref[0, g, :, lanes] += product


def partial_sums(z, distances, pattern, prior, weights, slope, coupling):
    per_plane = PLANE // PER_STEP
    count = len(distances)
    steps = jnp.concatenate(
        [((z + d) % ZN) * per_plane + jnp.arange(per_plane, dtype=jnp.int32) for d in distances]
    )
    out = pl.pallas_call(
        partial_kernel,
        grid_spec=pltpu.PrefetchScalarGridSpec(
            num_scalar_prefetch=2,
            grid=(count * per_plane,),
            in_specs=[
                pl.BlockSpec((CELL, WIDTH), lambda i, s, p: (0, 0)),
                pl.BlockSpec((1, WIDTH), lambda i, s, p: (0, 0)),
                pl.BlockSpec((None, PER_STEP, WIDTH), lambda i, s, p: (s[i], 0, 0)),
                pl.BlockSpec((SHELL, PER_STEP, BLK, BLK), lambda i, s, p: (0, s[i], 0, 0)),
            ],
            out_specs=pl.BlockSpec(
                (1, PER_STEP, CELL, WIDTH), lambda i, s, p: (i // per_plane, i % per_plane, 0, 0)
            ),
            scratch_shapes=[
                pltpu.VMEM((CELL, WIDTH), jnp.bfloat16),
                pltpu.VMEM((CELL, BLK), jnp.float32),
            ],
        ),
        out_shape=jax.ShapeDtypeStruct((count, PLANE, CELL, WIDTH), jnp.float32),
        cost_estimate=pl.CostEstimate(
            flops=2 * CELL * WIDTH * BLK * PLANE * count,
            bytes_accessed=count * PLANE * CELL * WIDTH * 4,
            transcendentals=0,
        ),
        name="partial_sums",
    )(steps, pattern, prior, weights, slope, coupling)
    return out


def powers_kernel(rate_ref, inscatter_ref, out_ref):
    row = lax.broadcasted_iota(jnp.int32, (BLK, BLK), 0)
    column = lax.broadcasted_iota(jnp.int32, (BLK, BLK), 1)
    unit = jnp.where(row == column, 1.0, 0.0).astype(jnp.float32)
    transfer = [unit + inscatter_ref[b] for b in range(SHELL)]
    now = list(transfer)
    for k in range(LAYERS):
        for b in range(SHELL):
            out_ref[b, k] = now[b]
            if k + 1 < LAYERS:
                now[b] = jnp.dot(
                    now[b] * rate_ref[:, pl.ds(b * BLK, BLK)],
                    transfer[b],
                    precision=HIGH,
                    preferred_element_type=jnp.float32,
                )


def last_kernel(direction_ref, source_ref, power_ref, out_ref):
    for b in range(SHELL):
        lanes = pl.ds(b * BLK, BLK)
        up = direction_ref[b] == 1
        total = jnp.zeros((LATERAL, BLK), jnp.float32)
        for t in range(LAYERS):
            k = jnp.where(up, LAYERS - 1 - t, t)
            total += jnp.dot(
                source_ref[pl.ds(t * LATERAL, LATERAL), lanes],
                power_ref[b, k],
                precision=HIGH,
                preferred_element_type=jnp.float32,
            )
        out_ref[:, lanes] = total


def particular_kernel(direction_ref, source_ref, rate_ref, power_ref, out_ref):
    now = [jnp.zeros((LATERAL, BLK), jnp.float32) for _ in range(SHELL)]
    for t in range(LAYERS):
        for b in range(SHELL):
            lanes = pl.ds(b * BLK, BLK)
            at = jnp.where(direction_ref[b] == 1, t, LAYERS - 1 - t)
            rows = pl.ds(pl.multiple_of(at * LATERAL, LATERAL), LATERAL)
            now[b] = jnp.dot(
                source_ref[rows, lanes] + rate_ref[:, lanes] * now[b],
                power_ref[b, 0],
                precision=HIGH,
                preferred_element_type=jnp.float32,
            )
            out_ref[rows, lanes] = now[b]


def finish_kernel(
    direction_ref, slab_ref, wall_ref, one_ref, two_ref, three_ref, rate_ref, particular_ref, power_ref, out_ref, faces
):
    for k, face in enumerate((one_ref, two_ref, three_ref)):
        faces[k] = face[...]
    slab = slab_ref[0]
    now = [wall_ref[:, pl.ds(b * BLK, BLK)] for b in range(SHELL)]
    for n in range(3):
        for b in range(SHELL):
            lanes = pl.ds(b * BLK, BLK)
            up = direction_ref[b] == 1
            k = jnp.where(up, 2 - n, n)
            active = jnp.where(up, (k + 1 <= slab).astype(jnp.int32), (k + 1 > slab).astype(jnp.int32))
            moved = faces[k, :, lanes] + jnp.dot(
                now[b] * rate_ref[:, lanes],
                power_ref[b, LAYERS - 1],
                precision=HIGH,
                preferred_element_type=jnp.float32,
            )
            now[b] = jnp.where(active == 1, moved, now[b])
    for b in range(SHELL):
        lanes = pl.ds(b * BLK, BLK)
        up = direction_ref[b] == 1
        scaled = now[b] * rate_ref[:, lanes]
        for t in range(LAYERS):
            k = jnp.where(up, t, LAYERS - 1 - t)
            rows = pl.ds(t * LATERAL, LATERAL)
            out_ref[rows, lanes] = particular_ref[rows, lanes] + jnp.dot(
                scaled, power_ref[b, k], precision=HIGH, preferred_element_type=jnp.float32
            )


SMEM = pl.BlockSpec(memory_space=pltpu.SMEM)
VMEM = pl.BlockSpec(memory_space=pltpu.VMEM)


def small_call(kernel, out_shape, specs, scratch=(), flops=0, name=None):
    return pl.pallas_call(
        kernel,
        in_specs=specs,
        out_specs=VMEM,
        out_shape=jax.ShapeDtypeStruct(out_shape, jnp.float32),
        scratch_shapes=list(scratch),
        cost_estimate=pl.CostEstimate(flops=flops, bytes_accessed=3 << 20, transcendentals=0),
        name=name,
    )


def per_device(
    occupation_prior,
    coupling,
    pattern,
    pseudo_weights,
    equilibrium_slope,
    direction,
    stream_rate,
    inscatter,
    inflow_low,
    inflow_high,
    front_of_row,
):
    modes = lax.axis_index("modes")
    slab = lax.axis_index("slab").astype(jnp.int32)
    z = (modes // PLANE).astype(jnp.int32)
    weights = pseudo_weights.reshape(1, WIDTH)
    rate = stream_rate.reshape(1, WIDTH)
    slope = equilibrium_slope.reshape(ZN * PLANE // PER_STEP, PER_STEP, WIDTH)
    make = functools.partial(
        partial_sums,
        pattern=pattern,
        prior=occupation_prior,
        weights=weights,
        slope=slope,
        coupling=coupling,
    )

    def reduced(distances):
        sums = make(z, distances)
        count = len(distances)
        if count > 1:
            sums = sums.swapaxes(0, 1)
        got = lax.psum_scatter(
            sums.reshape(PLANE * count * CELL, WIDTH),
            "modes",
            scatter_dimension=0,
            axis_index_groups=PLANES,
            tiled=True,
        )
        return [got[i * CELL : (i + 1) * CELL] for i in range(count)]

    (far,) = reduced((2,))
    (above,) = reduced((1,))
    (below,) = reduced((3,))
    (mine,) = reduced((0,))
    half = CELL // 2
    far_up = lax.ppermute(far[:half], "modes", z_route(1))
    far_down = lax.ppermute(far[half:], "modes", z_route(-1))
    above = jnp.concatenate([above[:half] + far_up, above[half:]], axis=0)
    below = jnp.concatenate([below[:half], below[half:] + far_down], axis=0)
    from_below = lax.ppermute(above, "modes", z_route(1))
    from_above = lax.ppermute(below, "modes", z_route(-1))
    source = mine + from_below + from_above

    powers = small_call(
        powers_kernel, (SHELL, LAYERS, BLK, BLK), [VMEM, VMEM], flops=200_000_000, name="powers"
    )(rate, inscatter)
    picks = front_of_row[:, None] == jnp.arange(inflow_low.shape[0], dtype=jnp.int32)[None, :]
    ahead = (jnp.repeat(direction, BLK) == 1)[None, :]
    inflow = jnp.where(ahead, inflow_low, inflow_high)
    wall = jnp.sum(jnp.where(picks[:, :, None], inflow[None, :, :], 0.0), axis=1)

    last = small_call(
        last_kernel, (LATERAL, WIDTH), [SMEM, VMEM, VMEM], flops=40_000_000, name="last_face"
    )(direction, source, powers)
    faces = [
        lax.ppermute(last, "slab", [(i, (i + k) % 4) for i in range(4)]) for k in (1, 2, 3)
    ]
    particular = small_call(
        particular_kernel, (CELL, WIDTH), [SMEM, VMEM, VMEM, VMEM], flops=40_000_000, name="particular"
    )(direction, source, rate, powers)
    return small_call(
        finish_kernel,
        (CELL, WIDTH),
        [SMEM, SMEM] + [VMEM] * 7,
        scratch=[pltpu.VMEM((3, LATERAL, WIDTH), jnp.float32)],
        flops=60_000_000,
        name="finish",
    )(direction, slab.reshape(1), wall, *faces, rate, particular, powers)


def solution(mesh):
    placed = (
        P("slab", "modes"),
        P("modes", None, None, None),
        P("modes", None),
        P("modes"),
        P(),
        P("modes"),
        P("modes"),
        P("modes", None, None),
        P(None, "modes"),
        P(None, "modes"),
        P(),
    )
    return jax.shard_map(
        per_device, mesh=mesh, in_specs=placed, out_specs=P("slab", "modes"), check_vma=False
    )
```

time: 552 us -> 387 us (0.70)
  blocking collectives: 188 us -> 0 us
  waiting for transfers between devices: 240 us -> 308 us
  Pallas kernels: 0 us -> 41.1 us
  local copies, waits for them, and re-layouts: 33.3 us -> 3.89 us
  other arithmetic: 29 us -> 6.49 us
  matrix products: 21.2 us -> 0 us
  starting transfers between devices: 25.3 us -> 14.4 us
    psum x1 -> x0, blocking collectives: 188 us -> none  [per_device(): pseudo_warmth_sum = lax.psum(branch_pseudo_warmth, 'modes')]
    reduce_scatter x1 -> x4, waiting for transfers between devices: 234 us -> 307 us  [reduced(): lax.psum_scatter(sums.reshape(PLANE * count * CELL, WIDTH), 'modes', scat...]
    pallas_call x0 -> x8, Pallas kernels: none -> 41.1 us  [the longest x4 24 us: partial_sums(): pl.pallas_call(partial_kernel, grid_spec=pltpu.PrefetchScalarGridSpec(num...]
    reduce_sum x2 -> x1, other arithmetic: 27.5 us -> 0.68 us  [per_device(): jnp.sum(jnp.where(picks[:, :, None], inflow[None, :, :], 0.0), axis=1)]
    dot_general x26 -> x0, matrix products: 21.2 us -> none  [the longest x8 7.65 us: local_sweep(): jnp.einsum('ybk,bkl->ybl', layer_source + rate_table * previous, transfer...]
    reduce_sum x1 -> x0, local copies, waits for them, and re-layouts: 17.5 us -> none  [per_device(): jnp.sum(jnp.where(selected[:, None, :, :, None], products[:, :, :, None,...]
    dot_general x1 -> x0, local copies, waits for them, and re-layouts: 11.7 us -> none  [per_device(): jnp.einsum('cbk,bgkl->bcgl', rounded, coupling, preferred_element_type=jn...]
    ppermute x6 -> x7, starting transfers between devices: 25.3 us -> 14.2 us  [the longest x3 4.02 us: per_device(): lax.ppermute(last, 'slab', [(i, (i + k) % 4) for i in range(4)])]
  transfers between devices with their start and end apart: 7 -> 11, of which waited for: 4 -> 4; matrix products, arithmetic and copies ran while one was open for 0% -> 1% of each run, Pallas kernels for 0% -> 7%
where the time goes in v1:
time: 387 us
  waiting for transfers between devices  308 us (80%)
  Pallas kernels  41.1 us (11%)
  starting transfers between devices  14.4 us (4%)
  between operations  13.3 us (3%)
  other arithmetic  6.49 us (2%)
  local copies, waits for them, and re-layouts  3.89 us (1%)
    reduce_scatter x4, waiting for transfers between devices, reduced(): lax.psum_scatter(sums.reshape(PLANE * count * CELL, WIDTH), 'modes', scat...  307 us
    pallas_call x4, Pallas kernels, partial_sums(): pl.pallas_call(partial_kernel, grid_spec=pltpu.PrefetchScalarGridSpec(num...  24 us
  transfers between devices with their start and end apart: 11, of which 4 were waited for; matrix products, arithmetic and copies ran while one was open for 1% of the time, Pallas kernels for 7%

profile of v1, /device:TPU:1, one launch (start us, length us, event | category | flops | bytes accessed | tf_op | source)
XLA Modules:
  0.0 386.6 jit_solution(2794576158641521838)
XLA Ops:
  6.5 0.5 iota_add_fusion.1.steps_ref
  7.0 1.6 reshape.56.slope_ref
  8.6 6.0 %partial_sums.6 = f32[1,16,128,512]{3,2,1,0:T(8,128)} custom-call(s32[4]{0:T(128)} %iota_add_fusion.1.steps_ref, s32[4,64]{1,0:T(4,128)} %pattern_ref.7, f32[128,512]{1,0:T(8,128)} %x_ref.7, f32[1,512]{1,0:T(1,128)} %bitcast.13, f32[16,4,512]{2,1,0:T(4,128)} %reshape.56.slope_ref, bf16[4,64,128,128]{3,2,1,0:T(8,128)(2,1)} %coupling_ref.7), custom_call_target="tpu_custom_call" | custom-call | flops 268435456 | bytes 4194304 | tf_op jit(solution)/shard_map/partial_sums/pallas_call | solution.py:62
  14.6 0.0 reduce-scatter.9.cloned.1.call-update
  14.6 0.0 reduce-scatter.7.cloned.1.call-start
  14.7 0.5 iota_add_fusion.2.steps_ref
  15.2 6.0 %partial_sums.5 = f32[1,16,128,512]{3,2,1,0:T(8,128)} custom-call(s32[4]{0:T(128)} %iota_add_fusion.2.steps_ref, s32[4,64]{1,0:T(4,128)} %pattern_ref.7, f32[128,512]{1,0:T(8,128)} %x_ref.7, f32[1,512]{1,0:T(1,128)} %bitcast.14, f32[16,4,512]{2,1,0:T(4,128)} %reshape.56.slope_ref, bf16[4,64,128,128]{3,2,1,0:T(8,128)(2,1)} %coupling_ref.7), custom_call_target="tpu_custom_call" | custom-call | flops 268435456 | bytes 4194304 | tf_op jit(solution)/shard_map/partial_sums/pallas_call | solution.py:62
  21.2 0.0 reduce-scatter.7.cloned.1.call-update
  21.2 0.0 reduce-scatter.11.cloned.1.call-start
  21.3 0.5 iota_add_fusion.steps_ref
  21.8 6.1 %partial_sums.7 = f32[1,16,128,512]{3,2,1,0:T(8,128)} custom-call(s32[4]{0:T(128)} %iota_add_fusion.steps_ref, s32[4,64]{1,0:T(4,128)} %pattern_ref.7, f32[128,512]{1,0:T(8,128)} %x_ref.7, f32[1,512]{1,0:T(1,128)} %bitcast.15, f32[16,4,512]{2,1,0:T(4,128)} %reshape.56.slope_ref, bf16[4,64,128,128]{3,2,1,0:T(8,128)(2,1)} %coupling_ref.7), custom_call_target="tpu_custom_call" | custom-call | flops 268435456 | bytes 4194304 | tf_op jit(solution)/shard_map/partial_sums/pallas_call | solution.py:62
  27.9 0.0 reduce-scatter.11.cloned.1.call-update
  27.9 0.0 reduce-scatter.5.cloned.1.call-start
  28.0 0.5 iota_add_fusion.3.steps_ref
  28.5 6.0 %partial_sums.4 = f32[1,16,128,512]{3,2,1,0:T(8,128)} custom-call(s32[4]{0:T(128)} %iota_add_fusion.3.steps_ref, s32[4,64]{1,0:T(4,128)} %pattern_ref.7, f32[128,512]{1,0:T(8,128)} %x_ref.7, f32[1,512]{1,0:T(1,128)} %bitcast.16, f32[16,4,512]{2,1,0:T(4,128)} %reshape.56.slope_ref, bf16[4,64,128,128]{3,2,1,0:T(8,128)(2,1)} %coupling_ref.7), custom_call_target="tpu_custom_call" | custom-call | flops 268435456 | bytes 4194304 | tf_op jit(solution)/shard_map/partial_sums/pallas_call | solution.py:62
  34.5 0.0 copy-start.4
  34.5 0.0 reduce-scatter.5.cloned.1.call-update
  34.5 0.6 copy-done.5
  35.2 65.3 %reduce-scatter.9.cloned.1.call-done = f32[128,512]{1,0:T(8,128)} async-done(((f32[2048,512]{1,0:T(8,128)}), f32[128,512]{1,0:T(8,128)}) %reduce-scatter.9.cloned.1.call-update) | async-done | bytes 262160 | tf_op jit(solution)/shard_map/reduce_scatter | solution.py:223
  100.4 1.0 fusion
  101.4 2.4 collective-permute-start
  103.8 0.1 broadcast_bitcast_fusion
  103.9 1.6 collective-permute-start.2
  105.5 81.6 %reduce-scatter.7.cloned.1.call-done = f32[128,512]{1,0:T(8,128)} async-done(((f32[2048,512]{1,0:T(8,128)}), f32[128,512]{1,0:T(8,128)}) %reduce-scatter.7.cloned.1.call-update) | async-done | bytes 262160 | tf_op jit(solution)/shard_map/reduce_scatter | solution.py:223
  187.1 0.0 collective-permute-done
  187.1 1.0 slice_add_fusion.1
  188.1 2.3 collective-permute-start.1
  190.4 83.1 %reduce-scatter.11.cloned.1.call-done = f32[128,512]{1,0:T(8,128)} async-done(((f32[2048,512]{1,0:T(8,128)}), f32[128,512]{1,0:T(8,128)}) %reduce-scatter.11.cloned.1.call-update) | async-done | bytes 262160 | tf_op jit(solution)/shard_map/reduce_scatter | solution.py:223
  273.6 0.0 collective-permute-done.2
  273.6 1.0 fusion.1
  274.6 3.9 %collective-permute-start.3 = (f32[128,512]{1,0:T(8,128)S(1)}, f32[128,512]{1,0:T(8,128)S(1)}, u32[]{:S(2)}, u32[]{:S(2)}) collective-permute-start(f32[128,512]{1,0:T(8,128)S(1)} %pad_maximum_fusion.1), channel_id=1, source_target_pairs={{0,48},{1,49},{2,50},{3,51},{4,52},{5,53},{6,54},{7,55},{8,56},{9,... | collective-permute-start | bytes 786440 | tf_op jit(solution)/shard_map/ppermute | solution.py:242
  278.5 4.0 %powers.1.power_ref = f32[4,8,128,128]{3,2,1,0:T(8,128)} custom-call(f32[1,512]{1,0:T(1,128)} %bitcast.17, f32[4,128,128]{2,1,0:T(8,128)} %inscatter_ref.1), custom_call_target="tpu_custom_call" | custom-call | flops 200000000 | bytes 3145728 | tf_op jit(solution)/shard_map/powers/pallas_call | solution.py:245
  282.5 77.4 %reduce-scatter.5.cloned.1.call-done = f32[128,512]{1,0:T(8,128)} async-done(((f32[2048,512]{1,0:T(8,128)}), f32[128,512]{1,0:T(8,128)}) %reduce-scatter.5.cloned.1.call-update) | async-done | bytes 262160 | tf_op jit(solution)/shard_map/reduce_scatter | solution.py:223
  359.9 0.0 collective-permute-done.1
  359.9 0.0 collective-permute-done.3
  359.9 1.7 add_add_fusion.source_ref
  361.7 4.1 %last_face.1 = f32[16,512]{1,0:T(8,128)} custom-call(s32[4]{0:T(128)} %direction_ref.5, f32[128,512]{1,0:T(8,128)} %add_add_fusion.source_ref, f32[4,8,128,128]{3,2,1,0:T(8,128)} %powers.1.power_ref), custom_call_target="tpu_custom_call" | custom-call | flops 40000000 | bytes 3145728 | tf_op jit(solution)/shard_map/last_face/pallas_call | solution.py:253
  365.7 3.6 collective-permute-start.4
  369.3 0.2 collective-permute-start.5
  369.5 0.2 collective-permute-start.6
  369.7 0.7 select_reduce_fusion.wall_ref
  370.4 4.2 %particular.1.particular_ref = f32[128,512]{1,0:T(8,128)} custom-call(s32[4]{0:T(128)} %direction_ref.5, f32[128,512]{1,0:T(8,128)} %add_add_fusion.source_ref, f32[1,512]{1,0:T(1,128)} %bitcast.18, f32[4,8,128,128]{3,2,1,0:T(8,128)} %powers.1.power_ref), custom_call_target="tpu_custom_call" | custom-call | flops 40000000 | bytes 3145728 | tf_op jit(solution)/shard_map/particular/pallas_call | solution.py:259
  374.6 0.0 collective-permute-done.4.one_ref
  374.6 0.0 collective-permute-done.6.three_ref
  374.6 0.6 copy-done
  375.2 0.0 copy-done.1
  375.2 0.0 copy-done.2
  375.2 4.8 %finish.1 = f32[128,512]{1,0:T(8,128)} custom-call(s32[4]{0:T(128)} %direction_ref.5, s32[1]{0:T(128)} %bitcast.slab_ref, f32[16,512]{1,0:T(8,128)} %select_reduce_fusion.wall_ref, f32[16,512]{1,0:T(8,128)} %copy-done, f32[16,512]{1,0:T(8,128)} %copy-done.1, f32[16,512]{1,0:T(8,128)} %copy-done.2, f32[1,512]{1,0:T(1,128)} %bitcast.19, ...), custom_call_target="tpu_custom_call" | custom-call | flops 60000000 | bytes 3145728 | tf_op jit(solution)/shard_map/finish/pallas_call | solution.py:262
  (16 shorter events, 0.1 us)
Async XLA Ops:
  6.5 93.9 %reduce-scatter.9.cloned.1.call-start = ((), (), s32[]{:S(2)}) async-start(), calls=%async_computation.6 | async-start | bytes 4456448 | tf_op jit(solution)/shard_map/reduce_scatter | solution.py:223
  14.6 172.4 %reduce-scatter.7.cloned.1.call-start = ((), (), s32[]{:S(2)}) async-start(), calls=%async_computation.5 | async-start | bytes 4456448 | tf_op jit(solution)/shard_map/reduce_scatter | solution.py:223
  21.2 252.4 %reduce-scatter.11.cloned.1.call-start = ((), (), s32[]{:S(2)}) async-start(), calls=%async_computation.7 | async-start | bytes 4456448 | tf_op jit(solution)/shard_map/reduce_scatter | solution.py:223
  27.9 332.0 %reduce-scatter.5.cloned.1.call-start = ((), (), s32[]{:S(2)}) async-start(), calls=%async_computation.4 | async-start | bytes 4456448 | tf_op jit(solution)/shard_map/reduce_scatter | solution.py:223
  34.5 0.7 copy-start.5
  34.5 244.0 %copy-start.6 = (s32[16]{0:T(128)S(1)}, s32[16]{0:T(128)}, u32[]{:S(2)}) copy-start(s32[16]{0:T(128)} %param.21) | copy-start | bytes 196
  34.5 248.0 %copy-start.3 = (f32[4,512]{1,0:T(4,128)S(1)}, f32[4,512]{1,0:T(4,128)}, u32[]{:S(2)}) copy-start(f32[4,512]{1,0:T(4,128)} %param.19) | copy-start | bytes 24580
  34.5 248.0 %copy-start.4 = (f32[4,512]{1,0:T(4,128)S(1)}, f32[4,512]{1,0:T(4,128)}, u32[]{:S(2)}) copy-start(f32[4,512]{1,0:T(4,128)} %param.20) | copy-start | bytes 24580
  101.4 85.6 %collective-permute-start = (f32[64,512]{1,0:T(8,128)S(1)}, f32[64,512]{1,0:T(8,128)S(1)}, u32[]{:S(2)}, u32[]{:S(2)}) collective-permute-start(f32[64,512]{1,0:T(8,128)S(1)} %get-tuple-element.7), channel_id=1, source_target_pairs={{0,16},{1,17},{2,18},{3,19},{4,20},{5,21},{6,22},{7,23},{8,24},{9,... | collective-permute-start | bytes 393224 | tf_op jit(solution)/shard_map/ppermute | solution.py:237
  103.9 169.7 %collective-permute-start.2 = (f32[64,512]{1,0:T(8,128)S(1)}, f32[64,512]{1,0:T(8,128)S(1)}, u32[]{:S(2)}, u32[]{:S(2)}) collective-permute-start(f32[64,512]{1,0:T(8,128)S(1)} %get-tuple-element.8), channel_id=1, source_target_pairs={{0,48},{1,49},{2,50},{3,51},{4,52},{5,53},{6,54},{7,55},{8,56},{9,... | collective-permute-start | bytes 393224 | tf_op jit(solution)/shard_map/ppermute | solution.py:238
  188.1 171.8 %collective-permute-start.1 = (f32[128,512]{1,0:T(8,128)S(1)}, f32[128,512]{1,0:T(8,128)S(1)}, u32[]{:S(2)}, u32[]{:S(2)}) collective-permute-start(f32[128,512]{1,0:T(8,128)S(1)} %pad_maximum_fusion), channel_id=1, source_target_pairs={{0,16},{1,17},{2,18},{3,19},{4,20},{5,21},{6,22},{7,23},{8,24},{9,... | collective-permute-start | bytes 786440 | tf_op jit(solution)/shard_map/ppermute | solution.py:241
  274.6 85.3 %collective-permute-start.3 = (f32[128,512]{1,0:T(8,128)S(1)}, f32[128,512]{1,0:T(8,128)S(1)}, u32[]{:S(2)}, u32[]{:S(2)}) collective-permute-start(f32[128,512]{1,0:T(8,128)S(1)} %pad_maximum_fusion.1), channel_id=1, source_target_pairs={{0,48},{1,49},{2,50},{3,51},{4,52},{5,53},{6,54},{7,55},{8,56},{9,... | collective-permute-start | bytes 786440 | tf_op jit(solution)/shard_map/ppermute | solution.py:242
  365.7 8.9 %collective-permute-start.4 = (f32[16,512]{1,0:T(8,128)}, f32[16,512]{1,0:T(8,128)S(1)}, u32[]{:S(2)}, u32[]{:S(2)}) collective-permute-start(f32[16,512]{1,0:T(8,128)} %last_face.1), channel_id=1, source_target_pairs={{0,64},{64,128},{128,192},{192,0},{1,65},{65,129},{129,193},{193,1... | collective-permute-start | bytes 98312 | tf_op jit(solution)/shard_map/ppermute | solution.py:257
  369.3 5.3 %collective-permute-start.5 = (f32[16,512]{1,0:T(8,128)}, f32[16,512]{1,0:T(8,128)S(1)}, u32[]{:S(2)}, u32[]{:S(2)}) collective-permute-start(f32[16,512]{1,0:T(8,128)} %last_face.1), channel_id=1, source_target_pairs={{0,128},{64,192},{128,0},{192,64},{1,129},{65,193},{129,1},{193,65... | collective-permute-start | bytes 98312 | tf_op jit(solution)/shard_map/ppermute | solution.py:257
  369.5 5.1 %collective-permute-start.6 = (f32[16,512]{1,0:T(8,128)}, f32[16,512]{1,0:T(8,128)S(1)}, u32[]{:S(2)}, u32[]{:S(2)}) collective-permute-start(f32[16,512]{1,0:T(8,128)} %last_face.1), channel_id=1, source_target_pairs={{0,192},{64,0},{128,64},{192,128},{1,193},{65,1},{129,65},{193,129... | collective-permute-start | bytes 98312 | tf_op jit(solution)/shard_map/ppermute | solution.py:257
  374.6 0.6 copy-start
  374.6 0.6 copy-start.1
  374.6 0.6 copy-start.2
Sparse Core Ops, SparseCore 0:
  14.7 85.6 reduce-scatter.8
  104.1 82.9 reduce-scatter.6
  190.7 82.8 reduce-scatter.10
  277.1 82.8 reduce-scatter.4
